TPU v7x, 32 devices: a whole 2x2x4 slice. The times are simulated.
32 devices in a mesh: replica: 8 (over y, x, core), shard: 4 (over z).
Axes of the slice: x: 2, y: 2, z: 4, core: 2. Of those that a mesh axis runs over, the one named last changes fastest.
Arguments:
- deltas: bfloat16 [8, 131072], P('replica', 'shard'), may hold values from -6 to 6
- counts: int32 [4], replicated, may hold values from 1000 to 8999, as said below
- momentum: float32 [262144], P(('shard', 'replica')), may hold values from -4 to 4
- params: bfloat16 [262144], P(('shard', 'replica')), may hold values from -6 to 6
Outputs:
- new_momentum: float32 [262144], P(('shard', 'replica'))
- new_params: bfloat16 [262144], P('shard')
Inputs may be any that keep to these rules, and one draw needn't show every extreme that they name: `counts`: tokens processed by each worker.
All inputs are finite; a program needn't handle non-finite values.
Results may differ from a plain program's by a relative error of at most 0.001.
Values may be sent and summed in bfloat16 or wider, within the bound.
A program may use at most 64 MiB of HBM per device.

v0:
```python
import jax
import jax.numpy as jnp
from jax import lax
from jax.sharding import PartitionSpec as P

momentum_rate = 0.9
outer_rate = 0.7


def local(deltas, counts, momentum, params):
    devices_axis = lax.axis_size("replica")
    workers = devices_axis // 2
    shares = counts.astype(jnp.float32)
    shares = shares / jnp.sum(shares)
    piece_len = momentum.shape[0]
    position = lax.axis_index("replica")
    own_half = position % 2
    halves = jnp.arange(2, dtype=jnp.int32)[:, None, None]
    placed = jnp.where(
        halves == own_half, deltas[0].reshape(1, workers, piece_len), jnp.zeros((), jnp.bfloat16)
    )
    blocks = placed.reshape(devices_axis, 1, piece_len)
    sender_shares = jnp.repeat(shares, 2)
    summed = jnp.sum(
        sender_shares[:, None, None]
        * lax.all_to_all(blocks, "replica", split_axis=0, concat_axis=0, tiled=True).astype(
            jnp.float32
        ),
        axis=0,
    )
    outer_grad = summed.reshape(piece_len)
    new_momentum = momentum_rate * momentum + outer_grad
    updated = (
        params.astype(jnp.float32) - outer_rate * (outer_grad + momentum_rate * new_momentum)
    ).astype(jnp.bfloat16)
    new_params = lax.all_gather(updated, "replica", axis=0, tiled=True)
    return (new_momentum, new_params)


def solution(mesh):
    placed = (P("replica", "shard"), P(), P(("shard", "replica")), P(("shard", "replica")))
    return jax.shard_map(
        local,
        mesh=mesh,
        in_specs=placed,
        out_specs=(P(("shard", "replica")), P("shard")),
        check_vma=False,
    )
```

profile of v0, /device:TPU:0, one launch (start us, length us, event | category | flops | bytes accessed | tf_op | source)
XLA Modules:
  0.0 25.5 jit_solution(7479907933899090309)
XLA Ops:
  0.7 0.1 broadcast_in_dim.33
  0.7 0.1 broadcast_in_dim.34
  0.8 1.3 %reduce.1 = bf16[32768]{0:T(1024)(128)(2,1)S(1)} reduce(bf16[1,32768]{1,0:T(2,128)(2,1)} %param.4, bf16[]{:T(256)} %constant.28), dimensions={0}, to_apply=%param.4.reduce_sub_computation | reduce | bytes 131074 | tf_op args[0]
  2.2 0.1 broadcast_select_fusion
  2.3 0.5 %broadcast.38 = bf16[]{:T(256)} broadcast(bf16[]{:T(256)} %constant.28), dimensions={} | broadcast | bytes 4 | tf_op jit(solution)/shard_map/jit(_where)/select_n | solution.py:19
  2.8 0.7 %reduce.2 = bf16[8,8192]{1,0:T(8,128)(2,1)S(1)} reduce(bf16[8,1,8192]{2,0,1:T(8,128)(2,1)S(1)} %broadcast_select_fusion, bf16[]{:T(256)} %broadcast.38), dimensions={1}, to_apply=%copy.6.reduce_sub_computation | reduce | bytes 262146 | tf_op jit(solution)/shard_map/jit(_where)/select_n | solution.py:19
  3.5 0.7 %reshape.52 = bf16[8,2,4096]{2,1,0:T(2,128)(2,1)} reshape(bf16[8,8192]{1,0:T(8,128)(2,1)S(1)} %reduce.2) | data formatting | bytes 262144
  4.2 0.0 copy-start.2
  4.2 5.3 %all-to-all-start = ((bf16[8,2,4096]{2,1,0:T(2,128)(2,1)}), bf16[8,2,4096]{2,1,0:T(2,128)(2,1)S(1)}, u32[]{:S(2)}, u32[]{:S(2)}) async-start(bf16[8,2,4096]{2,1,0:T(2,128)(2,1)} %reshape.52), calls=%async_computation | async-start | bytes 262144 | tf_op jit(solution)/shard_map/all_to_all | solution.py:26
  9.5 0.0 copy-done.2
  9.5 0.6 %convert_reduce_fusion = f32[]{:T(128)} fusion(s32[4]{0:T(128)S(1)} %copy-done.2), kind=kLoop, calls=%fused_computation.6 | loop fusion | flops 7 | bytes 20 | tf_op jit(solution)/shard_map/reduce_sum | solution.py:14
  10.1 0.6 %convert_divide_fusion = f32[4]{0:T(128)S(1)} fusion(s32[4]{0:T(128)S(1)} %copy-done.2, f32[]{:T(128)} %convert_reduce_fusion), kind=kLoop, calls=%fused_computation.5 | loop fusion | flops 8 | bytes 36 | tf_op jit(solution)/shard_map/div | solution.py:14
  10.8 0.1 broadcast_in_dim.32
  10.9 0.1 mul.23
  11.0 4.1 %all-to-all-done = bf16[8,2,4096]{2,1,0:T(2,128)(2,1)S(1)} async-done(((bf16[8,2,4096]{2,1,0:T(2,128)(2,1)}), bf16[8,2,4096]{2,1,0:T(2,128)(2,1)S(1)}, u32[]{:S(2)}, u32[]{:S(2)}) %all-to-all-start) | async-done | bytes 131104 | tf_op jit(solution)/shard_map/all_to_all | solution.py:26
  15.0 0.1 reshape.53
  15.2 0.0 copy-start
  15.2 0.0 copy-start.1
  15.2 0.4 %multiply_reduce_fusion = f32[8192]{0:T(1024)S(1)} fusion(bf16[8,1,8192]{2,1,0:T(2,128)(2,1)S(1)} %reshape.53, f32[8]{0:T(128)S(1)} %mul.23), kind=kLoop, calls=%fused_computation | loop fusion | flops 188416 | bytes 163872 | tf_op jit(solution)/shard_map/reduce_sum | solution.py:24
  15.6 0.3 %copy-done = f32[8192]{0:T(1024)S(1)} copy-done((f32[8192]{0:T(1024)S(1)}, f32[8192]{0:T(1024)}, u32[]{:S(2)}) %copy-start) | copy-done | bytes 32792
  15.9 0.0 copy-done.1
  15.9 0.6 %subtract_convert_fusion = (bf16[8192]{0:T(1024)(128)(2,1)S(1)}, f32[8192]{0:T(1024)}) fusion(f32[8192]{0:T(1024)S(1)} %multiply_reduce_fusion, bf16[8192]{0:T(1024)(128)(2,1)S(1)} %copy-done.1, f32[8192]{0:T(1024)S(1)} %copy-done), kind=kLoop, calls=%fused_computation.2 | loop fusion | flops 65536 | bytes 131072 | tf_op jit(solution)/shard_map/convert_element_type | solution.py:35
  16.6 8.2 %all_gather.3 = bf16[65536]{0:T(1024)(128)(2,1)S(1)} all-gather(bf16[8192]{0:T(1024)(128)(2,1)S(1)} %get-tuple-element.2), channel_id=1, replica_groups=mesh['replica'=8,'shard'=4] {'replica'}, dimensions={0}, use_global_device_ids=true | all-gather | bytes 147456 | tf_op jit(solution)/shard_map/all_gather | solution.py:36
  24.8 0.7 %copy.9 = bf16[65536]{0:T(1024)(128)(2,1)} copy(bf16[65536]{0:T(1024)(128)(2,1)S(1)} %all_gather.3) | data formatting | bytes 262144
  (4 shorter events, 0.1 us)
Async XLA Ops:
  4.2 5.3 %copy-start.2 = (s32[4]{0:T(128)S(1)}, s32[4]{0:T(128)}, u32[]{:S(2)}) copy-start(s32[4]{0:T(128)} %param.5) | copy-start | bytes 52
  4.2 10.8 %all-to-all-start = ((bf16[8,2,4096]{2,1,0:T(2,128)(2,1)}), bf16[8,2,4096]{2,1,0:T(2,128)(2,1)S(1)}, u32[]{:S(2)}, u32[]{:S(2)}) async-start(bf16[8,2,4096]{2,1,0:T(2,128)(2,1)} %reshape.52), calls=%async_computation | async-start | bytes 262144 | tf_op jit(solution)/shard_map/all_to_all | solution.py:26
  15.2 0.8 %copy-start = (f32[8192]{0:T(1024)S(1)}, f32[8192]{0:T(1024)}, u32[]{:S(2)}) copy-start(f32[8192]{0:T(1024)} %param.6) | copy-start | bytes 98308
  15.2 0.8 %copy-start.1 = (bf16[8192]{0:T(1024)(128)(2,1)S(1)}, bf16[8192]{0:T(1024)(128)(2,1)}, u32[]{:S(2)}) copy-start(bf16[8192]{0:T(1024)(128)(2,1)} %param.7) | copy-start | bytes 49156
where the time goes:
time: 25.8 us; the launch traced here: 25.5 us
  blocking collectives  8.25 us (32%)
  starting transfers between devices  5.33 us (21%)
  other arithmetic  4.29 us (17%)
  waiting for transfers between devices  4.08 us (16%)
  local copies, waits for them, and re-layouts  2.79 us (11%)
  between operations  0.72 us (3%)
    all_gather x1, blocking collectives, local(): new_params = lax.all_gather(updated, 'replica', axis=0, tiled=True)  8.25 us
    all_to_all x1, starting transfers between devices, local(): lax.all_to_all(blocks, 'replica', split_axis=0, concat_axis=0, tiled=True)  5.33 us
    all_to_all x1, waiting for transfers between devices, local(): lax.all_to_all(blocks, 'replica', split_axis=0, concat_axis=0, tiled=True)  4.08 us
    unnamed x9, local copies, waits for them, and re-layouts  1.86 us
    unnamed x1, other arithmetic  1.26 us
    select_n x2, other arithmetic, local(): jnp.where(halves == own_half, deltas[0].reshape(1, workers, piece_len), j...  0.75 us
    div x1, other arithmetic, local(): shares = shares / jnp.sum(shares)  0.65 us
    convert_element_type x1, other arithmetic, local(): updated = (params.astype(jnp.float32) - outer_rate * (outer_grad + moment...  0.62 us
  transfers between devices with their start and end apart: 1, of which 1 were waited for; matrix products, arithmetic and copies ran while one was open for 6% of the time, Pallas kernels for 0%

commit v1 on v0

v1 whole, which is shorter than its diff:
```python
import functools

import jax
import jax.numpy as jnp
from jax import lax
from jax.experimental import pallas as pl
from jax.experimental.pallas import tpu as pltpu
from jax.sharding import PartitionSpec as P

momentum_rate = 0.9
outer_rate = 0.7
LANES = 128


def kernel(
    n, rows, deltas_ref, counts_ref, momentum_ref, params_ref, new_momentum_ref, new_params_ref,
    raw, packed, arrived, mom, par, updated,
    in_sems, own_sem, send_sems, recv_sems, out_send_sems, out_recv_sems,
):
    workers = n // 2
    me = lax.axis_index("replica")
    worker = me // 2
    half = me % 2
    my_half = me // workers

    load_deltas = pltpu.make_async_copy(deltas_ref, raw, in_sems.at[0])
    load_momentum = pltpu.make_async_copy(momentum_ref, mom, in_sems.at[1])
    load_params = pltpu.make_async_copy(params_ref, par, in_sems.at[2])
    load_deltas.start()
    load_momentum.start()
    load_params.start()

    barrier = pltpu.get_barrier_semaphore()
    for step in range(1, n):
        pl.semaphore_signal(
            barrier, inc=1, device_id={"replica": lax.rem(me + step, n)},
            device_id_type=pl.DeviceIdType.MESH,
        )

    load_deltas.wait()
    wide = raw[...].astype(jnp.float32)
    packed[...] = wide.reshape(workers * rows, LANES).astype(jnp.bfloat16)
    pl.semaphore_wait(barrier, n - 1)

    def piece(q):
        return packed.at[pl.ds(pl.multiple_of(q * rows, rows), rows)]

    def slot(r):
        return arrived.at[pl.ds(pl.multiple_of(r * rows, rows), rows)]

    def send(step):
        q = lax.rem(worker + step, workers)
        return half * workers + q, pltpu.make_async_remote_copy(
            src_ref=piece(q), dst_ref=slot(worker), send_sem=send_sems.at[step],
            recv_sem=recv_sems.at[worker], device_id={"replica": half * workers + q},
            device_id_type=pl.DeviceIdType.MESH,
        )

    own = half == my_half
    own_piece = lax.rem(me, workers)
    own_copy = pltpu.make_async_copy(piece(own_piece), slot(worker), own_sem)
    for step in range(workers):
        target, copy = send(step)

        @pl.when(target != me)
        def _():
            copy.start()

    @pl.when(own)
    def _():
        own_copy.start()

    total = counts_ref[0].astype(jnp.float32)
    for r in range(1, workers):
        total = total + counts_ref[r].astype(jnp.float32)
    load_momentum.wait()
    load_params.wait()
    for r in range(workers):
        source = 2 * r + my_half
        recv = pltpu.make_async_remote_copy(
            src_ref=piece(0), dst_ref=slot(r), send_sem=send_sems.at[0],
            recv_sem=recv_sems.at[r], device_id={"replica": source},
            device_id_type=pl.DeviceIdType.MESH,
        )

        @pl.when(source != me)
        def _():
            recv.wait_recv()

        @pl.when(source == me)
        def _():
            own_copy.wait()

    grad = jnp.zeros((rows, LANES), jnp.float32)
    for r in range(workers):
        share = counts_ref[r].astype(jnp.float32) / total
        grad = grad + share * arrived[pl.ds(r * rows, rows)].astype(jnp.float32)
    new_momentum = momentum_rate * mom[...] + grad
    value = (
        par[...].astype(jnp.float32) - outer_rate * (grad + momentum_rate * new_momentum)
    ).astype(jnp.bfloat16)
    updated[...] = value
    new_momentum_ref[...] = new_momentum
    place = pl.ds(pl.multiple_of(me * rows, rows), rows)

    def gather(step):
        return pltpu.make_async_remote_copy(
            src_ref=updated, dst_ref=new_params_ref.at[place], send_sem=out_send_sems.at[step],
            recv_sem=out_recv_sems.at[me], device_id={"replica": lax.rem(me + step, n)},
            device_id_type=pl.DeviceIdType.MESH,
        )

    for step in range(1, n):
        gather(step).start()
    new_params_ref[place] = value

    for step in range(workers):
        target, copy = send(step)

        @pl.when(target != me)
        def _():
            copy.wait_send()

    for step in range(1, n):
        gather(step).wait_send()
    for step in range(1, n):
        source = lax.rem(me + step, n)
        pltpu.make_async_remote_copy(
            src_ref=updated,
            dst_ref=new_params_ref.at[pl.ds(pl.multiple_of(source * rows, rows), rows)],
            send_sem=out_send_sems.at[step], recv_sem=out_recv_sems.at[source],
            device_id={"replica": source}, device_id_type=pl.DeviceIdType.MESH,
        ).wait_recv()


def local(deltas, counts, momentum, params):
    n = lax.axis_size("replica")
    workers = n // 2
    piece_len = momentum.shape[0]
    rows = piece_len // LANES
    new_momentum, new_params = pl.pallas_call(
        functools.partial(kernel, n, rows),
        out_shape=(
            jax.ShapeDtypeStruct((rows, LANES), jnp.float32),
            jax.ShapeDtypeStruct((n * rows, LANES), jnp.bfloat16),
        ),
        in_specs=[
            pl.BlockSpec(memory_space=pl.ANY),
            pl.BlockSpec(memory_space=pltpu.SMEM),
            pl.BlockSpec(memory_space=pl.ANY),
            pl.BlockSpec(memory_space=pl.ANY),
        ],
        out_specs=(
            pl.BlockSpec(memory_space=pltpu.VMEM),
            pl.BlockSpec(memory_space=pltpu.VMEM),
        ),
        scratch_shapes=[
            pltpu.VMEM((1, workers * piece_len), jnp.bfloat16),
            pltpu.VMEM((workers * rows, LANES), jnp.bfloat16),
            pltpu.VMEM((workers * rows, LANES), jnp.bfloat16),
            pltpu.VMEM((rows, LANES), jnp.float32),
            pltpu.VMEM((rows, LANES), jnp.bfloat16),
            pltpu.VMEM((rows, LANES), jnp.bfloat16),
            pltpu.SemaphoreType.DMA((3,)),
            pltpu.SemaphoreType.DMA,
            pltpu.SemaphoreType.DMA((workers,)),
            pltpu.SemaphoreType.DMA((workers,)),
            pltpu.SemaphoreType.DMA((n,)),
            pltpu.SemaphoreType.DMA((n,)),
        ],
        compiler_params=pltpu.CompilerParams(collective_id=0, has_side_effects=True),
    )(deltas, counts, momentum.reshape(rows, LANES), params.reshape(rows, LANES))
    return new_momentum.reshape(piece_len), new_params.reshape(n * piece_len)


def solution(mesh):
    placed = (P("replica", "shard"), P(), P(("shard", "replica")), P(("shard", "replica")))
    return jax.shard_map(
        local,
        mesh=mesh,
        in_specs=placed,
        out_specs=(P(("shard", "replica")), P("shard")),
        check_vma=False,
    )
```

time: 25.8 us -> 15.4 us (0.60)
  Pallas kernels: 0 us -> 11.6 us
  blocking collectives: 8.25 us -> 0 us
  starting transfers between devices: 5.33 us -> 0 us
  other arithmetic: 4.29 us -> 0 us
  waiting for transfers between devices: 4.08 us -> 0 us
    pallas_call x0 -> x1, Pallas kernels: none -> 11.6 us  [local(): pl.pallas_call(functools.partial(kernel, n, rows), out_shape=(jax.ShapeDt...]
    all_gather x1 -> x0, blocking collectives: 8.25 us -> none  [local(): new_params = lax.all_gather(updated, 'replica', axis=0, tiled=True)]
    all_to_all x1 -> x0, starting transfers between devices: 5.33 us -> none  [local(): lax.all_to_all(blocks, 'replica', split_axis=0, concat_axis=0, tiled=True)]
    all_to_all x1 -> x0, waiting for transfers between devices: 4.08 us -> none  [local(): lax.all_to_all(blocks, 'replica', split_axis=0, concat_axis=0, tiled=True)]
    unnamed x1 -> x0, other arithmetic: 1.26 us -> none
    unnamed x9 -> x2, local copies, waits for them, and re-layouts: 1.86 us -> 2.94 us
    reduce_sum x2 -> x0, other arithmetic: 1 us -> none  [the longest x1 0.6 us: local(): shares = shares / jnp.sum(shares)]
    select_n x2 -> x0, other arithmetic: 0.75 us -> none  [local(): jnp.where(halves == own_half, deltas[0].reshape(1, workers, piece_len), j...]
  transfers between devices with their start and end apart: 1 -> 0, of which waited for: 1 -> 0; matrix products, arithmetic and copies ran while one was open for 6% -> 0% of each run, Pallas kernels for 0% -> 0%
where the time goes in v1:
time: 15.4 us; the launch traced here: 15.2 us
  Pallas kernels  11.6 us (75%)
  local copies, waits for them, and re-layouts  2.94 us (19%)
  between operations  0.64 us (4%)
    pallas_call x1, Pallas kernels, local(): pl.pallas_call(functools.partial(kernel, n, rows), out_shape=(jax.ShapeDt...  11.6 us
    unnamed x2, local copies, waits for them, and re-layouts  2.94 us

profile of v1, /device:TPU:0, one launch (start us, length us, event | category | flops | bytes accessed | tf_op | source)
XLA Modules:
  0.0 15.2 jit_solution(1455336710509934921)
XLA Ops:
  0.6 11.6 %shard_map.59 = (f32[64,128]{1,0:T(8,128)}, bf16[512,128]{1,0:T(8,128)(2,1)}) custom-call(bf16[1,32768]{1,0:T(2,128)(2,1)} %deltas_ref.1, s32[4]{0:T(128)} %counts_ref.1, f32[64,128]{1,0:T(8,128)} %bitcast.6, bf16[64,128]{1,0:T(8,128)(2,1)} %bitcast.7), custom_call_target="tpu_custom_call" | custom-call | tf_op jit(solution)/shard_map/pallas_call | solution.py:141
  12.2 1.4 %copy.8 = f32[8192]{0:T(1024)} copy(f32[8192]{0:T(1024)} %bitcast.5) | data formatting | bytes 65536
  13.6 1.6 %copy.9 = bf16[65536]{0:T(1024)(128)(2,1)} copy(bf16[65536]{0:T(1024)(128)(2,1)} %bitcast.4) | data formatting | bytes 262144

commit v2 on v1

--- a/solution.py
+++ b/solution.py
@@ -133,6 +133,15 @@
         ).wait_recv()
 
 
+def write_out(momentum_ref, params_ref, new_momentum_ref, new_params_ref, sems):
+    first = pltpu.make_async_copy(params_ref, new_params_ref, sems.at[0])
+    second = pltpu.make_async_copy(momentum_ref, new_momentum_ref, sems.at[1])
+    first.start()
+    second.start()
+    second.wait()
+    first.wait()
+
+
 def local(deltas, counts, momentum, params):
     n = lax.axis_size("replica")
     workers = n // 2
@@ -141,8 +150,8 @@
     new_momentum, new_params = pl.pallas_call(
         functools.partial(kernel, n, rows),
         out_shape=(
-            jax.ShapeDtypeStruct((rows, LANES), jnp.float32),
-            jax.ShapeDtypeStruct((n * rows, LANES), jnp.bfloat16),
+            pltpu.VMEM((rows, LANES), jnp.float32),
+            pltpu.VMEM((n * rows, LANES), jnp.bfloat16),
         ),
         in_specs=[
             pl.BlockSpec(memory_space=pl.ANY),
@@ -170,6 +179,19 @@
         ],
         compiler_params=pltpu.CompilerParams(collective_id=0, has_side_effects=True),
     )(deltas, counts, momentum.reshape(rows, LANES), params.reshape(rows, LANES))
+    new_momentum, new_params = pl.pallas_call(
+        write_out,
+        out_shape=(
+            jax.ShapeDtypeStruct((rows, LANES), jnp.float32),
+            jax.ShapeDtypeStruct((n * rows, LANES), jnp.bfloat16),
+        ),
+        in_specs=[pl.BlockSpec(memory_space=pltpu.VMEM)] * 2,
+        out_specs=(pl.BlockSpec(memory_space=pl.ANY),) * 2,
+        scratch_shapes=[pltpu.SemaphoreType.DMA((2,))],
+    )(
+        pltpu.with_memory_space_constraint(new_momentum, pltpu.VMEM),
+        pltpu.with_memory_space_constraint(new_params, pltpu.VMEM),
+    )
     return new_momentum.reshape(piece_len), new_params.reshape(n * piece_len)
 
 

time: 15.4 us -> 12.4 us (0.81)
  local copies, waits for them, and re-layouts: 2.94 us -> 0 us
    unnamed x2 -> x0, local copies, waits for them, and re-layouts: 2.94 us -> none
    pallas_call x1 -> x2, Pallas kernels: 11.6 us -> 11.6 us  [the longest x1 10.9 us: local(): pl.pallas_call(functools.partial(kernel, n, rows), out_shape=(pltpu.VMEM(...]
where the time goes in v2:
time: 12.4 us; the launch traced here: 12.3 us
  Pallas kernels  11.6 us (94%)
  between operations  0.64 us (5%)
    pallas_call x1, Pallas kernels, local(): pl.pallas_call(functools.partial(kernel, n, rows), out_shape=(pltpu.VMEM(...  10.9 us
    pallas_call x1, Pallas kernels, local(): pl.pallas_call(write_out, out_shape=(jax.ShapeDtypeStruct((rows, LANES),...  0.68 us

profile of v2, /device:TPU:0, one launch (start us, length us, event | category | flops | bytes accessed | tf_op | source)
XLA Modules:
  0.0 12.3 jit_solution(15491444013709509430)
XLA Ops:
  0.6 10.9 %shard_map.59 = (f32[64,128]{1,0:T(8,128)S(1)}, bf16[512,128]{1,0:T(8,128)(2,1)S(1)}) custom-call(bf16[1,32768]{1,0:T(2,128)(2,1)} %deltas_ref.1, s32[4]{0:T(128)} %counts_ref.1, f32[64,128]{1,0:T(8,128)} %bitcast.4, bf16[64,128]{1,0:T(8,128)(2,1)} %bitcast.5), custom_call_target="tpu_custom_call" | custom-call | tf_op jit(solution)/shard_map/pallas_call | solution.py:150
  11.6 0.7 %shard_map.60 = (f32[64,128]{1,0:T(8,128)}, bf16[512,128]{1,0:T(8,128)(2,1)}) custom-call(f32[64,128]{1,0:T(8,128)S(1)} %get-tuple-element.6.momentum_ref, bf16[512,128]{1,0:T(8,128)(2,1)S(1)} %get-tuple-element.7.params_ref), custom_call_target="tpu_custom_call" | custom-call | tf_op jit(solution)/shard_map/pallas_call | solution.py:182

commit v3 on v2

v3 whole, which is shorter than its diff:
```python
import functools

import jax
import jax.numpy as jnp
from jax import lax
from jax.experimental import pallas as pl
from jax.experimental.pallas import tpu as pltpu
from jax.sharding import PartitionSpec as P

momentum_rate = 0.9
outer_rate = 0.7
LANES = 128
CHUNKS = 1


def flipped(index, mask):
    bit = 1
    while bit <= mask:
        if mask & bit:
            index = index + bit * (1 - 2 * (index // bit % 2))
        bit *= 2
    return index


def far_first(count):
    return sorted(range(count), key=lambda mask: -bin(mask >> 1).count("1"))


def kernel(
    n, rows, deltas_ref, counts_ref, momentum_ref, params_ref, new_momentum_ref, new_params_ref,
    counts, raw, packed, arrived, mom, par,
    in_sems, send_sems, recv_sems, out_send_sems, out_recv_sems,
):
    workers = n // 2
    part = rows // CHUNKS
    me = lax.axis_index("replica")
    worker = me // 2
    half = me % 2
    my_half = me // workers
    my_piece = me % workers

    load_deltas = pltpu.make_async_copy(deltas_ref, raw, in_sems.at[0])
    load_momentum = pltpu.make_async_copy(momentum_ref, mom, in_sems.at[1])
    load_params = pltpu.make_async_copy(params_ref, par, in_sems.at[2])
    load_counts = pltpu.make_async_copy(counts_ref, counts, in_sems.at[3])
    barrier = pltpu.get_barrier_semaphore()
    for mask in far_first(n):
        if mask:
            pl.semaphore_signal(
                barrier, inc=1, device_id={"replica": flipped(me, mask)},
                device_id_type=pl.DeviceIdType.MESH,
            )
    load_deltas.start()
    load_counts.start()
    load_momentum.start()
    load_params.start()

    load_deltas.wait()
    wide = raw[...].astype(jnp.float32)
    packed[...] = wide.reshape(workers * rows, LANES).astype(jnp.bfloat16)

    def span(block, chunk):
        return pl.ds(pl.multiple_of(block * rows + chunk * part, part), part)

    @pl.when(half == my_half)
    def _():
        for chunk in range(CHUNKS):
            arrived[span(worker, chunk)] = packed[span(my_piece, chunk)]

    load_counts.wait()
    total = counts[0].astype(jnp.float32)
    for r in range(1, workers):
        total = total + counts[r].astype(jnp.float32)
    shares = [
        jnp.full((1, LANES), counts[r].astype(jnp.float32)) / jnp.full((1, LANES), total)
        for r in range(workers)
    ]
    load_momentum.wait()
    load_params.wait()
    pl.semaphore_wait(barrier, n - 1)

    def send(mask, chunk):
        q = flipped(my_piece, mask)
        target = half * workers + q
        return target, pltpu.make_async_remote_copy(
            src_ref=packed.at[span(q, chunk)], dst_ref=arrived.at[span(worker, chunk)],
            send_sem=send_sems.at[chunk, mask], recv_sem=recv_sems.at[chunk, worker],
            device_id={"replica": target}, device_id_type=pl.DeviceIdType.MESH,
        )

    def gather(mask, chunk):
        target = flipped(me, mask)
        return pltpu.make_async_remote_copy(
            src_ref=new_params_ref.at[span(me, chunk)], dst_ref=new_params_ref.at[span(me, chunk)],
            send_sem=out_send_sems.at[chunk, mask], recv_sem=out_recv_sems.at[chunk, mask],
            device_id={"replica": target}, device_id_type=pl.DeviceIdType.MESH,
        )

    def landing(mask, chunk):
        source = flipped(me, mask)
        return pltpu.make_async_remote_copy(
            src_ref=new_params_ref.at[span(source, chunk)],
            dst_ref=new_params_ref.at[span(source, chunk)],
            send_sem=out_send_sems.at[chunk, mask], recv_sem=out_recv_sems.at[chunk, mask],
            device_id={"replica": source}, device_id_type=pl.DeviceIdType.MESH,
        )

    for chunk in range(CHUNKS):
        for mask in far_first(workers):
            target, copy = send(mask, chunk)
            if mask:
                copy.start()
            else:

                @pl.when(target != me)
                def _():
                    copy.start()

    for chunk in range(CHUNKS):
        for r in range(workers):
            source = 2 * r + my_half

            @pl.when(source != me)
            def _():
                pltpu.make_async_remote_copy(
                    src_ref=packed.at[span(0, chunk)], dst_ref=arrived.at[span(r, chunk)],
                    send_sem=send_sems.at[chunk, 0], recv_sem=recv_sems.at[chunk, r],
                    device_id={"replica": source}, device_id_type=pl.DeviceIdType.MESH,
                ).wait_recv()

        grad = jnp.zeros((part, LANES), jnp.float32)
        for r in range(workers):
            grad = grad + shares[r] * arrived[span(r, chunk)].astype(jnp.float32)
        own = pl.ds(chunk * part, part)
        new_momentum = momentum_rate * mom[own] + grad
        new_params_ref[span(me, chunk)] = (
            par[own].astype(jnp.float32) - outer_rate * (grad + momentum_rate * new_momentum)
        ).astype(jnp.bfloat16)
        new_momentum_ref[own] = new_momentum
        for mask in far_first(n):
            if mask:
                gather(mask, chunk).start()

    for chunk in range(CHUNKS):
        for mask in far_first(workers):
            target, copy = send(mask, chunk)

            @pl.when(target != me)
            def _():
                copy.wait_send()

    for chunk in range(CHUNKS):
        for mask in range(1, n):
            gather(mask, chunk).wait_send()
    for chunk in range(CHUNKS):
        for mask in range(1, n):
            landing(mask, chunk).wait_recv()


def write_out(momentum_ref, params_ref, new_momentum_ref, new_params_ref, sems):
    first = pltpu.make_async_copy(params_ref, new_params_ref, sems.at[0])
    second = pltpu.make_async_copy(momentum_ref, new_momentum_ref, sems.at[1])
    first.start()
    second.start()
    second.wait()
    first.wait()


def local(deltas, counts, momentum, params):
    n = lax.axis_size("replica")
    workers = n // 2
    piece_len = momentum.shape[0]
    rows = piece_len // LANES
    new_momentum, new_params = pl.pallas_call(
        functools.partial(kernel, n, rows),
        out_shape=(
            pltpu.VMEM((rows, LANES), jnp.float32),
            pltpu.VMEM((n * rows, LANES), jnp.bfloat16),
        ),
        in_specs=[
            pl.BlockSpec(memory_space=pl.ANY),
            pl.BlockSpec(memory_space=pl.ANY),
            pl.BlockSpec(memory_space=pl.ANY),
            pl.BlockSpec(memory_space=pl.ANY),
        ],
        out_specs=(
            pl.BlockSpec(memory_space=pltpu.VMEM),
            pl.BlockSpec(memory_space=pltpu.VMEM),
        ),
        scratch_shapes=[
            pltpu.SMEM((workers,), jnp.int32),
            pltpu.VMEM((1, workers * piece_len), jnp.bfloat16),
            pltpu.VMEM((workers * rows, LANES), jnp.bfloat16),
            pltpu.VMEM((workers * rows, LANES), jnp.bfloat16),
            pltpu.VMEM((rows, LANES), jnp.float32),
            pltpu.VMEM((rows, LANES), jnp.bfloat16),
            pltpu.SemaphoreType.DMA((4,)),
            pltpu.SemaphoreType.DMA((CHUNKS, workers)),
            pltpu.SemaphoreType.DMA((CHUNKS, workers)),
            pltpu.SemaphoreType.DMA((CHUNKS, n)),
            pltpu.SemaphoreType.DMA((CHUNKS, n)),
        ],
        compiler_params=pltpu.CompilerParams(collective_id=0, has_side_effects=True),
    )(deltas, counts, momentum.reshape(rows, LANES), params.reshape(rows, LANES))
    new_momentum, new_params = pl.pallas_call(
        write_out,
        out_shape=(
            jax.ShapeDtypeStruct((rows, LANES), jnp.float32),
            jax.ShapeDtypeStruct((n * rows, LANES), jnp.bfloat16),
        ),
        in_specs=[pl.BlockSpec(memory_space=pltpu.VMEM)] * 2,
        out_specs=(pl.BlockSpec(memory_space=pl.ANY),) * 2,
        scratch_shapes=[pltpu.SemaphoreType.DMA((2,))],
    )(
        pltpu.with_memory_space_constraint(new_momentum, pltpu.VMEM),
        pltpu.with_memory_space_constraint(new_params, pltpu.VMEM),
    )
    return new_momentum.reshape(piece_len), new_params.reshape(n * piece_len)


def solution(mesh):
    placed = (P("replica", "shard"), P(), P(("shard", "replica")), P(("shard", "replica")))
    return jax.shard_map(
        local,
        mesh=mesh,
        in_specs=placed,
        out_specs=(P(("shard", "replica")), P("shard")),
        check_vma=False,
    )
```

time: 12.4 us -> 11.7 us (0.944)
  Pallas kernels: 11.6 us -> 10.9 us
    pallas_call x1, Pallas kernels: 10.9 us -> 10.2 us  [local(): pl.pallas_call(functools.partial(kernel, n, rows), out_shape=(pltpu.VMEM(...]
where the time goes in v3:
time: 11.7 us; the launch traced here: 11.6 us
  Pallas kernels  10.9 us (93%)
  between operations  0.64 us (5%)
    pallas_call x1, Pallas kernels, local(): pl.pallas_call(functools.partial(kernel, n, rows), out_shape=(pltpu.VMEM(...  10.2 us
    pallas_call x1, Pallas kernels, local(): pl.pallas_call(write_out, out_shape=(jax.ShapeDtypeStruct((rows, LANES),...  0.68 us

profile of v3, /device:TPU:0, one launch (start us, length us, event | category | flops | bytes accessed | tf_op | source)
XLA Modules:
  0.0 11.6 jit_solution(11195362844701555464)
XLA Ops:
  0.6 10.2 %shard_map.59 = (f32[64,128]{1,0:T(8,128)S(1)}, bf16[512,128]{1,0:T(8,128)(2,1)S(1)}) custom-call(bf16[1,32768]{1,0:T(2,128)(2,1)} %deltas_ref.1, s32[4]{0:T(128)} %counts_ref.1, f32[64,128]{1,0:T(8,128)} %bitcast.4, bf16[64,128]{1,0:T(8,128)(2,1)} %bitcast.5), custom_call_target="tpu_custom_call" | custom-call | tf_op jit(solution)/shard_map/pallas_call | solution.py:174
  10.9 0.7 %shard_map.60 = (f32[64,128]{1,0:T(8,128)}, bf16[512,128]{1,0:T(8,128)(2,1)}) custom-call(f32[64,128]{1,0:T(8,128)S(1)} %get-tuple-element.6.momentum_ref, bf16[512,128]{1,0:T(8,128)(2,1)S(1)} %get-tuple-element.7.params_ref), custom_call_target="tpu_custom_call" | custom-call | tf_op jit(solution)/shard_map/pallas_call | solution.py:205

commit v4 on v3

--- a/solution.py
+++ b/solution.py
@@ -72,8 +72,9 @@
     for r in range(1, workers):
         total = total + counts[r].astype(jnp.float32)
     shares = [
-        jnp.full((1, LANES), counts[r].astype(jnp.float32)) / jnp.full((1, LANES), total)
-        for r in range(workers)
+        jnp.full((1, LANES), counts[flipped(worker, mask)].astype(jnp.float32))
+        / jnp.full((1, LANES), total)
+        for mask in range(workers)
     ]
     load_momentum.wait()
     load_params.wait()
@@ -116,21 +117,28 @@
                 def _():
                     copy.start()
 
-    for chunk in range(CHUNKS):
-        for r in range(workers):
-            source = 2 * r + my_half
-
-            @pl.when(source != me)
-            def _():
-                pltpu.make_async_remote_copy(
-                    src_ref=packed.at[span(0, chunk)], dst_ref=arrived.at[span(r, chunk)],
-                    send_sem=send_sems.at[chunk, 0], recv_sem=recv_sems.at[chunk, r],
-                    device_id={"replica": source}, device_id_type=pl.DeviceIdType.MESH,
-                ).wait_recv()
-
+    def arrival(mask, chunk):
+        r = flipped(worker, mask)
+        return pltpu.make_async_remote_copy(
+            src_ref=packed.at[span(0, chunk)], dst_ref=arrived.at[span(r, chunk)],
+            send_sem=send_sems.at[chunk, 0], recv_sem=recv_sems.at[chunk, r],
+            device_id={"replica": 2 * r + my_half}, device_id_type=pl.DeviceIdType.MESH,
+        )
+
+    for chunk in range(CHUNKS):
         grad = jnp.zeros((part, LANES), jnp.float32)
-        for r in range(workers):
-            grad = grad + shares[r] * arrived[span(r, chunk)].astype(jnp.float32)
+        for mask in sorted(range(workers), key=lambda mask: bin(mask).count("1")):
+            if mask:
+                arrival(mask, chunk).wait_recv()
+            else:
+
+                @pl.when(half != my_half)
+                def _():
+                    arrival(0, chunk).wait_recv()
+
+            grad = grad + shares[mask] * arrived[
+                span(flipped(worker, mask), chunk)
+            ].astype(jnp.float32)
         own = pl.ds(chunk * part, part)
         new_momentum = momentum_rate * mom[own] + grad
         new_params_ref[span(me, chunk)] = (

time: 11.7 us -> 11.7 us (level)
  no operation moved by 1% of the time
where the time goes in v4:
time: 11.7 us; the launch traced here: 11.6 us
  Pallas kernels  10.9 us (93%)
  between operations  0.64 us (5%)
    pallas_call x1, Pallas kernels, local(): pl.pallas_call(functools.partial(kernel, n, rows), out_shape=(pltpu.VMEM(...  10.2 us
    pallas_call x1, Pallas kernels, local(): pl.pallas_call(write_out, out_shape=(jax.ShapeDtypeStruct((rows, LANES),...  0.68 us

profile of v4, /device:TPU:0, one launch (start us, length us, event | category | flops | bytes accessed | tf_op | source)
XLA Modules:
  0.0 11.6 jit_solution(2700828900553035201)
XLA Ops:
  0.6 10.2 %shard_map.59 = (f32[64,128]{1,0:T(8,128)S(1)}, bf16[512,128]{1,0:T(8,128)(2,1)S(1)}) custom-call(bf16[1,32768]{1,0:T(2,128)(2,1)} %deltas_ref.1, s32[4]{0:T(128)} %counts_ref.1, f32[64,128]{1,0:T(8,128)} %bitcast.4, bf16[64,128]{1,0:T(8,128)(2,1)} %bitcast.5), custom_call_target="tpu_custom_call" | custom-call | tf_op jit(solution)/shard_map/pallas_call | solution.py:182
  10.9 0.7 %shard_map.60 = (f32[64,128]{1,0:T(8,128)}, bf16[512,128]{1,0:T(8,128)(2,1)}) custom-call(f32[64,128]{1,0:T(8,128)S(1)} %get-tuple-element.6.momentum_ref, bf16[512,128]{1,0:T(8,128)(2,1)S(1)} %get-tuple-element.7.params_ref), custom_call_target="tpu_custom_call" | custom-call | tf_op jit(solution)/shard_map/pallas_call | solution.py:213
